TPU v7x, 32 devices: a whole 2x2x4 slice. The times are simulated.
32 devices in a mesh: shard: 2 (over y), ctx: 4 (over z), tp: 4 (over x, core).
Axes of the slice: x: 2, y: 2, z: 4, core: 2. Of those that a mesh axis runs over, the one named last changes fastest.
Arguments:
- inputs: bfloat16 [2, 4096, 768], P('shard', 'ctx'), may hold values from -6 to 6
- lengths: int32 [2], P('shard'), may hold values from 1024 to 4096, as said below
- global_blocks: int32 [2, 2], P('shard'), may hold values from 0 to 15, as said below
- random_blocks: int32 [2, 64, 3], P('shard', 'ctx'), may hold values from 0 to 63
- master_blocks: float32 [768, 96, 96], P(('shard', 'ctx', 'tp'))
- outer_vectors: float32 [6, 768], replicated
- inner_biases: float32 [4, 1152], P('tp'), may hold values from -4 to 4
- left_stats: float32 [768, 96, 96], P(('shard', 'ctx', 'tp')), as said below
- right_stats: float32 [768, 96, 96], P(('shard', 'ctx', 'tp')), as said below
- left_roots: float32 [768, 96, 96], P(('shard', 'ctx', 'tp')), as said below
- right_roots: float32 [768, 96, 96], P(('shard', 'ctx', 'tp')), as said below
- cotangent: bfloat16 [2, 4096, 768], P('shard', 'ctx'), may hold values from -6 to 6
Outputs:
- output: bfloat16 [2, 4096, 768], P('shard', 'ctx')
- input_grad: bfloat16 [2, 4096, 768], P('shard', 'ctx')
- block_grads: float32 [768, 96, 96], P(('shard', 'ctx', 'tp'))
- outer_grads: float32 [6, 768], P(None, ('shard', 'ctx'))
- inner_grads: float32 [4, 1152], P('tp', ('shard', 'ctx'))
- maxima: float32 [12], P('tp')
- left_new: float32 [768, 96, 96], P(('shard', 'ctx', 'tp'))
- right_new: float32 [768, 96, 96], P(('shard', 'ctx', 'tp'))
- new_blocks: float32 [768, 96, 96], P(('shard', 'ctx', 'tp'))
- new_outer: float32 [6, 768], P(None, ('shard', 'ctx'))
- new_inner: float32 [4, 1152], P('tp', ('shard', 'ctx'))
Inputs may be any that keep to these rules, and one draw needn't show every extreme that they name: `lengths`: sequence 0 holds 4096 valid tokens. `global_blocks`: the two ids of a sequence differ. `left_stats`: each block is symmetric. `right_stats`: each block is symmetric. `left_roots`: each block is symmetric. `right_roots`: each block is symmetric.
All inputs are finite; a program needn't handle non-finite values.
Results may differ from a plain program's by a relative error of at most 0.018.
Values may be sent and summed in bfloat16 or wider, within the bound.
No kernel may reach another device: no remote copies, remote signals or barrier semaphores. Data moves between devices by JAX's collectives and lax.ppermute only.
A program may use at most 192 MiB of HBM per device.

v0:
```python
import jax
import jax.numpy as jnp
from jax import lax
from jax.sharding import PartitionSpec as P

D = 768
HEADS = 12
HEAD = 64
FF = 3072
BLOCK = 64
SEQ = 4096
PB = 96
eps_norm = 1e-06
tau_clip = 9.0
rate_matrix = 0.3
rate_vector = 0.001
neg_large = -1e30
high = lax.Precision.HIGHEST


def layer_norm(values, gain, shift):
    mean_val = jnp.mean(values, axis=-1, keepdims=True)
    centred = values - mean_val
    var_val = jnp.mean(centred * centred, axis=-1, keepdims=True)
    return centred * lax.rsqrt(var_val + eps_norm) * gain + shift


def gelu_tanh(values):
    return jax.nn.gelu(values, approximate=True)


def to_grid(blocks, row_count, col_count):
    shaped = blocks.reshape(row_count // PB, col_count // PB, PB, PB)
    return shaped.transpose(0, 2, 1, 3).reshape(row_count, col_count)


def from_grid(matrix):
    row_count, col_count = matrix.shape
    shaped = matrix.reshape(row_count // PB, PB, col_count // PB, PB)
    return shaped.transpose(0, 2, 1, 3).reshape(-1, PB, PB)


def unpack_weights(whole, head_cols, unit_count):
    first_end = D // PB * (3 * head_cols // PB)
    second_end = first_end + head_cols // PB * (D // PB)
    third_end = second_end + D // PB * (unit_count // PB)
    return (
        to_grid(whole[:first_end], D, 3 * head_cols),
        to_grid(whole[first_end:second_end], head_cols, D),
        to_grid(whole[second_end:third_end], D, unit_count),
        to_grid(whole[third_end:], unit_count, D),
    )


def block_layout(slot_length, global_ids, random_ids, first_block, rows_blocks, block_count):
    rows = first_block + jnp.arange(rows_blocks, dtype=jnp.int32)
    window = jnp.stack([rows - 1, rows, rows + 1], axis=1)
    globals_row = jnp.broadcast_to(global_ids[None, :], (rows_blocks, 2))
    listed = jnp.concatenate([window, globals_row, random_ids], axis=1)
    inside = (listed >= 0) & (listed < block_count)
    clipped = jnp.clip(listed, 0, block_count - 1)
    key_pos = listed[:, :, None] * BLOCK + jnp.arange(BLOCK, dtype=jnp.int32)[None, None, :]
    key_mask = (inside[:, :, None] & (key_pos < slot_length)).reshape(rows_blocks, -1)
    query_pos = (first_block * BLOCK + jnp.arange(rows_blocks * BLOCK, dtype=jnp.int32)).reshape(
        rows_blocks, BLOCK
    )
    return (clipped, key_mask, query_pos < slot_length)


def pick_blocks(full_rows, clipped, head_count):
    block_count = full_rows.shape[0] // BLOCK
    picked = full_rows.reshape(block_count, BLOCK, -1)[clipped]
    return picked.reshape(clipped.shape[0], clipped.shape[1] * BLOCK, head_count, HEAD)


def attend_scores(query_blocks, key_blocks):
    return jnp.einsum(
        "lqhd,lkhd->lhqk", query_blocks, key_blocks, preferred_element_type=jnp.float32
    ) * HEAD ** (-0.5)


def probs_again(query_blocks, d_out_blocks, key_blocks, value_blocks, key_mask, lse_blk):
    raw_scores = attend_scores(query_blocks, key_blocks)
    probs = jnp.exp(jnp.where(key_mask[:, None, None, :], raw_scores, neg_large) - lse_blk)
    d_probs = jnp.einsum(
        "lqhd,lkhd->lhqk", d_out_blocks, value_blocks, preferred_element_type=jnp.float32
    )
    return (probs, d_probs)


def group_back(
    query_blocks,
    d_out_blocks,
    key_src,
    value_src,
    clipped,
    key_mask,
    lse_blk,
    delta_blk,
    block_count,
):
    rows_blocks, _, heads_here, _ = query_blocks.shape
    head_cols = heads_here * HEAD
    key_blocks = pick_blocks(key_src, clipped, heads_here)
    value_blocks = pick_blocks(value_src, clipped, heads_here)
    probs, d_probs = probs_again(
        query_blocks, d_out_blocks, key_blocks, value_blocks, key_mask, lse_blk
    )
    delta_blk = jnp.sum(probs * d_probs, axis=-1, keepdims=True)
    d_scores = (probs * (d_probs - delta_blk)).astype(jnp.bfloat16)
    d_query = jnp.einsum(
        "lhqk,lkhd->lqhd", d_scores, key_blocks, preferred_element_type=jnp.float32
    ) * HEAD ** (-0.5)
    d_key_blocks = jnp.einsum(
        "lhqk,lqhd->lkhd", d_scores, query_blocks, preferred_element_type=jnp.float32
    ) * HEAD ** (-0.5)
    d_value_blocks = jnp.einsum(
        "lhqk,lqhd->lkhd",
        probs.astype(jnp.bfloat16),
        d_out_blocks,
        preferred_element_type=jnp.float32,
    )
    listed_count = clipped.shape[1]
    d_key_full = (
        jnp.zeros((block_count, BLOCK, head_cols), jnp.float32)
        .at[clipped]
        .add(d_key_blocks.reshape(rows_blocks, listed_count, BLOCK, head_cols))
    )
    d_value_full = (
        jnp.zeros((block_count, BLOCK, head_cols), jnp.float32)
        .at[clipped]
        .add(d_value_blocks.reshape(rows_blocks, listed_count, BLOCK, head_cols))
    )
    return (
        d_query.reshape(-1, head_cols),
        d_key_full.reshape(-1, head_cols),
        d_value_full.reshape(-1, head_cols),
    )


def per_device(
    inputs,
    lengths,
    global_blocks,
    random_blocks,
    master_blocks,
    outer_vectors,
    inner_biases,
    left_stats,
    right_stats,
    left_roots,
    right_roots,
    cotangent,
):
    tensor_count = lax.axis_size("tp")
    owner_count = lax.axis_size(("shard", "ctx"))
    heads_here = HEADS // tensor_count
    head_cols = heads_here * HEAD
    unit_count = FF // tensor_count
    slot_count, ctx_tokens, _ = inputs.shape
    rows_blocks = ctx_tokens // BLOCK
    block_count = SEQ // BLOCK
    ctx_index = lax.axis_index("ctx")
    owner_index = lax.axis_index(("shard", "ctx"))
    gathered = lax.all_gather(
        master_blocks.astype(jnp.bfloat16), ("shard", "ctx"), axis=0, tiled=True
    )
    w_qkv, w_out, w_up, w_down = unpack_weights(gathered, head_cols, unit_count)
    flat_in = inputs.reshape(-1, D)
    inner_row = inner_biases[0]
    q_bias = inner_row[:head_cols]
    v_bias = inner_row[head_cols : 2 * head_cols]
    up_bias = inner_row[2 * head_cols :]
    projected = jnp.dot(flat_in, w_qkv, preferred_element_type=jnp.float32)
    queries = (projected[:, :head_cols] + q_bias).astype(jnp.bfloat16)
    key_rows = (
        projected[:, head_cols : 2 * head_cols]
        .astype(jnp.bfloat16)
        .reshape(slot_count, ctx_tokens, head_cols)
    )
    value_rows = (
        (projected[:, 2 * head_cols :] + v_bias)
        .astype(jnp.bfloat16)
        .reshape(slot_count, ctx_tokens, head_cols)
    )
    keys_all, values_all = (
        lax.all_gather(key_rows, "ctx", axis=1, tiled=True),
        lax.all_gather(value_rows, "ctx", axis=1, tiled=True),
    )
    query_slots = queries.reshape(slot_count, ctx_tokens, head_cols)
    peak_logit = jnp.full((heads_here,), neg_large, jnp.float32)
    slot_index = 0
    clipped, key_mask, query_mask = block_layout(
        lengths[slot_index],
        global_blocks[slot_index],
        random_blocks[slot_index],
        ctx_index * rows_blocks,
        rows_blocks,
        block_count,
    )
    layouts = [(clipped, key_mask)]
    query_blocks = query_slots[slot_index].reshape(rows_blocks, BLOCK, heads_here, HEAD)
    key_blocks = pick_blocks(keys_all[slot_index], clipped, heads_here)
    value_blocks = pick_blocks(values_all[slot_index], clipped, heads_here)
    raw_scores = attend_scores(query_blocks, key_blocks)
    both_mask = key_mask[:, None, None, :] & query_mask[:, None, :, None]
    peak_logit = jnp.maximum(
        peak_logit, jnp.max(jnp.where(both_mask, raw_scores, neg_large), axis=(0, 2, 3))
    )
    masked = jnp.where(key_mask[:, None, None, :], raw_scores, neg_large)
    row_top = jnp.max(masked, axis=-1, keepdims=True)
    shifted = jnp.exp(masked - row_top)
    row_total = jnp.sum(shifted, axis=-1, keepdims=True)
    probs = shifted / row_total
    lse_list = [row_top + jnp.log(row_total)]
    attended = jnp.einsum(
        "lhqk,lkhd->lqhd",
        probs.astype(jnp.bfloat16),
        value_blocks,
        preferred_element_type=jnp.float32,
    )
    attended_list = attended.reshape(ctx_tokens, head_cols)
    attended_low = attended_list.astype(jnp.bfloat16)
    branch = (
        lax.psum(jnp.dot(attended_low, w_out, preferred_element_type=jnp.float32), "tp")
        + outer_vectors[0]
    )
    hidden_in = flat_in.astype(jnp.float32) + branch
    x_first = layer_norm(hidden_in, outer_vectors[2], outer_vectors[3])
    x_first_low = x_first.astype(jnp.bfloat16)
    gate_pre = jnp.dot(x_first_low, w_up, preferred_element_type=jnp.float32) + up_bias
    act_low = gelu_tanh(gate_pre).astype(jnp.bfloat16)
    ff_out = (
        lax.psum(jnp.dot(act_low, w_down, preferred_element_type=jnp.float32), "tp")
        + outer_vectors[1]
    )
    mixed_sum = x_first + ff_out
    result = layer_norm(mixed_sum, outer_vectors[4], outer_vectors[5])
    maxima = lax.pmax(peak_logit, ("shard", "ctx"))
    positions = ctx_index * ctx_tokens + jnp.arange(ctx_tokens, dtype=jnp.int32)
    row_valid = (positions[None, :] < lengths[:, None]).astype(jnp.float32).reshape(-1)
    d_result = cotangent.reshape(-1, D).astype(jnp.float32) * row_valid[:, None]
    regathered = lax.all_gather(
        master_blocks.astype(jnp.bfloat16), ("shard", "ctx"), axis=0, tiled=True
    )
    wb_qkv, wb_out, wb_up, wb_down = unpack_weights(regathered, head_cols, unit_count)
    _, back_second = jax.vjp(layer_norm, mixed_sum, outer_vectors[4], outer_vectors[5])
    d_mixed, d_gain2, d_shift2 = back_second(d_result)
    d_ff_low = d_mixed.astype(jnp.bfloat16)
    d_bias2 = jnp.sum(d_ff_low.astype(jnp.float32), axis=0)
    g_down = jnp.dot(act_low.T, d_ff_low, preferred_element_type=jnp.float32)
    d_act = jnp.dot(d_ff_low, wb_down.T, preferred_element_type=jnp.float32)
    _, back_gelu = jax.vjp(gelu_tanh, gate_pre)
    d_gate_low = back_gelu(d_act)[0].astype(jnp.bfloat16)
    d_upbias = jnp.sum(d_gate_low.astype(jnp.float32), axis=0)
    g_up = jnp.dot(x_first_low.T, d_gate_low, preferred_element_type=jnp.float32)
    d_first = d_mixed + lax.psum(
        jnp.dot(d_gate_low, wb_up.T, preferred_element_type=jnp.float32), "tp"
    )
    _, back_first = jax.vjp(layer_norm, hidden_in, outer_vectors[2], outer_vectors[3])
    d_hidden, d_gain1, d_shift1 = back_first(d_first)
    d_branch_low = d_hidden.astype(jnp.bfloat16)
    d_bias_out = jnp.sum(d_branch_low.astype(jnp.float32), axis=0)
    g_out = jnp.dot(attended_low.T, d_branch_low, preferred_element_type=jnp.float32)
    d_att_low = jnp.dot(d_branch_low, wb_out.T, preferred_element_type=jnp.float32).astype(
        jnp.bfloat16
    )
    d_att_slots = d_att_low.reshape(slot_count, ctx_tokens, head_cols)
    keys_back, values_back = (keys_all, values_all)
    slot_index = 0
    clipped, key_mask = layouts[slot_index]
    query_blocks = query_slots[slot_index].reshape(rows_blocks, BLOCK, heads_here, HEAD)
    d_out_blocks = d_att_slots[slot_index].reshape(rows_blocks, BLOCK, heads_here, HEAD)
    d_query, d_key_full, d_value_full = group_back(
        query_blocks,
        d_out_blocks,
        keys_back[slot_index],
        values_back[slot_index],
        clipped,
        key_mask,
        lse_list[slot_index],
        None,
        block_count,
    )
    dk_list = [d_key_full]
    dv_list = [d_value_full]
    d_keys, d_values = (
        lax.psum_scatter(
            jnp.stack(dk_list).astype(jnp.bfloat16), "ctx", scatter_dimension=1, tiled=True
        ).astype(jnp.float32),
        lax.psum_scatter(
            jnp.stack(dv_list).astype(jnp.bfloat16), "ctx", scatter_dimension=1, tiled=True
        ).astype(jnp.float32),
    )
    d_q_low = d_query.astype(jnp.bfloat16)
    d_k_low = d_keys.reshape(-1, head_cols).astype(jnp.bfloat16)
    d_v_low = d_values.reshape(-1, head_cols).astype(jnp.bfloat16)
    d_proj = jnp.concatenate([d_q_low, d_k_low, d_v_low], axis=1)
    d_qbias = jnp.sum(d_q_low.astype(jnp.float32), axis=0)
    d_vbias = jnp.sum(d_v_low.astype(jnp.float32), axis=0)
    g_qkv = jnp.dot(flat_in.T, d_proj, preferred_element_type=jnp.float32)
    d_inputs = d_hidden + lax.psum(
        jnp.dot(d_proj, wb_qkv.T, preferred_element_type=jnp.float32).astype(jnp.bfloat16), "tp"
    ).astype(jnp.float32)
    input_grad = d_inputs.reshape(inputs.shape).astype(jnp.bfloat16)
    blocks_grad = jnp.concatenate(
        [from_grid(g_qkv), from_grid(g_out), from_grid(g_up), from_grid(g_down)], axis=0
    )
    outer_part = jnp.stack([d_bias_out, d_bias2, d_gain1, d_shift1, d_gain2, d_shift2], axis=0)
    inner_part = jnp.concatenate([d_qbias, d_vbias, d_upbias])[None, :]
    block_sum, outer_sum, inner_sum = (
        lax.psum_scatter(blocks_grad, ("shard", "ctx"), scatter_dimension=0, tiled=True),
        lax.psum_scatter(outer_part, ("shard", "ctx"), scatter_dimension=1, tiled=True),
        lax.psum_scatter(inner_part, ("shard", "ctx"), scatter_dimension=1, tiled=True),
    )
    left_new = 0.5 * left_stats + 0.5 * jnp.einsum(
        "bij,bkj->bik", block_sum, block_sum, precision=high
    )
    right_new = 0.5 * right_stats + 0.5 * jnp.einsum(
        "bji,bjk->bik", block_sum, block_sum, precision=high
    )
    left_applied = jnp.einsum("bij,bjk->bik", left_roots, block_sum, precision=high)
    step_val = jnp.einsum("bij,bjk->bik", left_applied, right_roots, precision=high)
    clip_sqrt = jnp.sqrt(tau_clip / jnp.maximum(maxima, tau_clip))
    head_factor = jnp.repeat(clip_sqrt, HEAD)
    table = jnp.concatenate([head_factor, head_factor, jnp.ones((head_cols,), jnp.float32)])
    qkv_factor = jnp.tile(table.reshape(1, -1, PB), (D // PB, 1, 1)).reshape(-1, PB)
    blocks_here = master_blocks.shape[0]
    all_factor = jnp.concatenate(
        [qkv_factor, jnp.ones((blocks_here * owner_count - qkv_factor.shape[0], PB), jnp.float32)],
        axis=0,
    )
    own_factor = lax.dynamic_slice_in_dim(all_factor, owner_index * blocks_here, blocks_here, 0)
    new_blocks = (master_blocks - rate_matrix * step_val) * own_factor[:, None, :]
    outer_cols = D // owner_count
    own_outer = lax.dynamic_slice_in_dim(outer_vectors, owner_index * outer_cols, outer_cols, 1)
    new_outer = own_outer - rate_vector * outer_sum
    inner_cols = inner_biases.shape[1] // owner_count
    inner_factor = jnp.concatenate([head_factor, jnp.ones((head_cols + unit_count,), jnp.float32)])
    own_inner_factor = lax.dynamic_slice_in_dim(
        inner_factor, owner_index * inner_cols, inner_cols, 0
    )
    own_inner = lax.dynamic_slice_in_dim(inner_biases, owner_index * inner_cols, inner_cols, 1)
    new_inner = (own_inner - rate_vector * inner_sum) * own_inner_factor[None, :]
    output = result.reshape(inputs.shape).astype(jnp.bfloat16)
    return (
        output,
        input_grad,
        block_sum,
        outer_sum,
        inner_sum,
        maxima,
        left_new,
        right_new,
        new_blocks,
        new_outer,
        new_inner,
    )


def solution(mesh):
    return jax.shard_map(
        per_device,
        mesh=mesh,
        in_specs=(
            P("shard", "ctx", None),
            P("shard"),
            P("shard", None),
            P("shard", "ctx", None),
            P(("shard", "ctx", "tp"), None, None),
            P(),
            P("tp", None),
            P(("shard", "ctx", "tp"), None, None),
            P(("shard", "ctx", "tp"), None, None),
            P(("shard", "ctx", "tp"), None, None),
            P(("shard", "ctx", "tp"), None, None),
            P("shard", "ctx", None),
        ),
        out_specs=(
            P("shard", "ctx", None),
            P("shard", "ctx", None),
            P(("shard", "ctx", "tp"), None, None),
            P(None, ("shard", "ctx")),
            P("tp", ("shard", "ctx")),
            P("tp"),
            P(("shard", "ctx", "tp"), None, None),
            P(("shard", "ctx", "tp"), None, None),
            P(("shard", "ctx", "tp"), None, None),
            P(None, ("shard", "ctx")),
            P("tp", ("shard", "ctx")),
        ),
        check_vma=False,
    )
```

profile of v0, /device:TPU:0, one launch (start us, length us, event | category | flops | bytes accessed | tf_op | source)
XLA Modules:
  0.0 1027.7 jit_solution(3224889106006550222)
XLA Ops:
  9.6 83.2 %all-gather.6.cloned.1.call-done = bf16[192,96,96]{2,1,0:T(8,128)(2,1)} async-done(((bf16[24,96,96]{2,1,0:T(8,128)(2,1)}), bf16[192,96,96]{2,1,0:T(8,128)(2,1)}) %all-gather.6.cloned.1.call-update) | async-done | bytes 3538960 | tf_op jit(solution)/shard_map/all_gather | solution.py:165
  109.1 27.4 %all-gather.10.cloned.1.call-done = bf16[4096,192]{0,1:T(8,128)(2,1)} async-done(((bf16[1024,192]{0,1:T(8,128)(2,1)}), bf16[4096,192]{0,1:T(8,128)(2,1)}) %all-gather.10.cloned.1.call-update) | async-done | bytes 1572880 | tf_op jit(solution)/shard_map/all_gather | solution.py:187
  142.4 15.9 %reshape.559 = bf16[16,512,3,64]{3,2,1,0:T(4,128)(2,1)} reshape(bf16[128,64,192]{2,1,0:T(8,128)(2,1)} %gather_fusion.1) | data formatting | bytes 6291456 | tf_op jit(solution)/shard_map/reshape | solution.py:73
  158.4 12.2 %copy.106 = bf16[16,512,3,64]{1,3,2,0:T(8,128)(2,1)} copy(bf16[16,512,3,64]{3,2,1,0:T(4,128)(2,1)} %reshape.559) | data formatting | bytes 6291456 | tf_op jit(solution)/shard_map/reshape | solution.py:73
  170.6 4.1 all-gather.8.cloned.1.call-done
  180.5 15.9 %reshape.558 = bf16[16,512,3,64]{3,2,1,0:T(4,128)(2,1)} reshape(bf16[128,64,192]{2,1,0:T(8,128)(2,1)} %gather_fusion) | data formatting | bytes 6291456 | tf_op jit(solution)/shard_map/reshape | solution.py:73
  196.4 12.3 %copy.107 = bf16[16,512,3,64]{1,3,2,0:T(8,128)(2,1)} copy(bf16[16,512,3,64]{3,2,1,0:T(4,128)(2,1)} %reshape.558) | data formatting | bytes 6291456 | tf_op jit(solution)/shard_map/reshape | solution.py:73
  233.3 3.9 reshape.490
  237.2 52.6 %all-reduce.7.cloned.1.call-done = f32[1024,768]{1,0:T(8,128)} async-done(((f32[1024,768]{1,0:T(8,128)}), f32[1024,768]{1,0:T(8,128)}) %all-reduce.7.cloned.1.call-update) | async-done | bytes 3145744 | tf_op jit(solution)/shard_map/psum | solution.py:225
  302.4 67.8 %all-reduce.9.cloned.1.call-done = f32[1024,768]{1,0:T(8,128)} async-done(((f32[1024,768]{1,0:T(8,128)}), f32[1024,768]{1,0:T(8,128)}) %all-reduce.9.cloned.1.call-update) | async-done | bytes 3145744 | tf_op jit(solution)/shard_map/psum | solution.py:234
  384.2 4.3 convert_reduce_fusion
  393.6 67.9 %all-reduce.11.cloned.1.call-done = f32[1024,768]{1,0:T(8,128)} async-done(((f32[1024,768]{1,0:T(8,128)}), f32[1024,768]{1,0:T(8,128)}) %all-reduce.11.cloned.1.call-update) | async-done | bytes 3145744 | tf_op jit(solution)/shard_map/psum | solution.py:257
  461.5 5.4 multiply_reduce_fusion.1
  473.4 7.2 fusion.20
  480.6 15.1 %copy.136 = f32[16,512,3,64]{3,2,1,0:T(4,128)} copy(f32[16,512,3,64]{1,3,2,0:T(8,128)} %fusion.20) | data formatting | bytes 12582912 | tf_op jit(solution)/shard_map/reshape | solution.py:132
  495.7 18.9 %reshape.553 = f32[128,64,192]{2,1,0:T(8,128)} reshape(f32[16,512,3,64]{3,2,1,0:T(4,128)} %copy.136) | data formatting | bytes 12582912 | tf_op jit(solution)/shard_map/reshape | solution.py:132
  517.0 26.2 %scatter_fusion.1 = f32[64,64,192]{2,1,0:T(8,128)} fusion(f32[64,64,192]{2,1,0:T(8,128)} %broadcast.358.clone, s32[128]{0:T(128)S(1)} %reshape.508, f32[128,64,192]{2,1,0:T(8,128)} %reshape.553), kind=kCustom, calls=%fused_computation.3 | custom fusion | flops 1572864 | bytes 18874880 | tf_op jit(solution)/shard_map/scatter-add | solution.py:132
  548.7 6.7 multiply_reduce_fusion
  564.5 15.1 %copy.135 = f32[16,512,3,64]{3,2,1,0:T(4,128)} copy(f32[16,512,3,64]{1,3,2,0:T(8,128)} %multiply_bitcast_fusion) | data formatting | bytes 12582912 | tf_op jit(solution)/shard_map/reshape | solution.py:127
  579.6 18.9 %reshape.552 = f32[128,64,192]{2,1,0:T(8,128)} reshape(f32[16,512,3,64]{3,2,1,0:T(4,128)} %copy.135) | data formatting | bytes 12582912 | tf_op jit(solution)/shard_map/reshape | solution.py:127
  601.0 26.2 %scatter_fusion = f32[64,64,192]{2,1,0:T(8,128)} fusion(f32[64,64,192]{2,1,0:T(8,128)} %broadcast.358.clone.1, s32[128]{0:T(128)S(1)} %reshape.508, f32[128,64,192]{2,1,0:T(8,128)} %reshape.552), kind=kCustom, calls=%fused_computation.2 | custom fusion | flops 1572864 | bytes 18874880 | tf_op jit(solution)/shard_map/scatter-add | solution.py:127
  632.7 4.3 fusion.58
  639.5 4.3 copy.127
  647.8 4.3 copy.126
  668.0 4.1 convolution_convert_fusion
  681.3 7.7 pad_maximum_fusion
  689.7 19.4 %pmax.7 = f32[3]{0:T(128)S(1)} all-reduce(f32[3]{0:T(128)S(1)} %broadcast_maximum_fusion), channel_id=1, replica_groups=mesh['shard'=2,'ctx'=4,'tp'=4] {'shard','ctx'}, use_global_device_ids=true, to_apply=%region_32.33 | all-reduce | flops 3 | bytes 24 | tf_op jit(solution)/shard_map/pmax | solution.py:239
  710.0 22.3 %reduce-scatter.16.cloned.1.call-done = f32[96,6]{1,0:T(8,128)} async-done(((f32[768,6]{1,0:T(8,128)}), f32[96,6]{1,0:T(8,128)}) %reduce-scatter.16.cloned.1.call-update) | async-done | bytes 2320
  734.6 63.3 %reduce-scatter.18.cloned.1.call-done = f32[144,1]{1,0:T(8,128)} async-done(((f32[1152,1]{1,0:T(8,128)}), f32[144,1]{1,0:T(8,128)}) %reduce-scatter.18.cloned.1.call-update) | async-done | bytes 592
  800.1 42.6 %all-reduce.13.cloned.1.call-done = bf16[1024,768]{1,0:T(8,128)(2,1)} async-done(((bf16[1024,768]{1,0:T(8,128)(2,1)}), bf16[1024,768]{1,0:T(8,128)(2,1)}) %all-reduce.13.cloned.1.call-update) | async-done | bytes 1572880 | tf_op jit(solution)/shard_map/psum | solution.py:302
  842.7 3.9 fusion.26
  846.7 162.3 %reduce-scatter.14.cloned.1.call-done = f32[24,96,96]{2,1,0:T(8,128)} async-done(((f32[192,96,96]{2,1,0:T(8,128)}), f32[24,96,96]{2,1,0:T(8,128)}) %reduce-scatter.14.cloned.1.call-update) | async-done | bytes 884752 | tf_op jit(solution)/shard_map/reduce_scatter | solution.py:312
  (317 shorter events, 166.3 us)
Async XLA Ops:
  7.2 1001.7 %copy-start = (f32[24,96,96]{2,1,0:T(8,128)S(1)}, f32[24,96,96]{2,1,0:T(8,128)}, u32[]{:S(2)}) copy-start(f32[24,96,96]{2,1,0:T(8,128)} %param.21) | copy-start | bytes 2654212
  7.2 85.6 %all-gather.6.cloned.1.call-start = ((), (), s32[]{:S(2)}) async-start(), calls=%async_computation.5 | async-start | bytes 5308416 | tf_op jit(solution)/shard_map/all_gather | solution.py:165
  9.5 127.0 %all-gather.10.cloned.1.call-start = ((), (), s32[]{:S(2)}) async-start(), calls=%async_computation.14 | async-start | bytes 1966080 | tf_op jit(solution)/shard_map/all_gather | solution.py:187
  100.9 6.9 slice-start.1
  101.0 73.7 %all-gather.8.cloned.1.call-start = ((), (), s32[]{:S(2)}) async-start(), calls=%async_computation.13 | async-start | bytes 1966080 | tf_op jit(solution)/shard_map/all_gather | solution.py:188
  103.4 186.4 %all-reduce.7.cloned.1.call-start = ((), (), s32[]{:S(2)}) async-start(), calls=%async_computation.6 | async-start | bytes 6291456 | tf_op jit(solution)/shard_map/psum | solution.py:225
  196.4 12.3 %copy-start.12 = (bf16[16,64,3,64]{1,0,3,2:T(8,128)(2,1)S(1)}, bf16[16,64,3,64]{1,0,3,2:T(8,128)(2,1)}, u32[]{:S(2)}) copy-start(bf16[16,64,3,64]{1,0,3,2:T(8,128)(2,1)} %reshape_squeeze_reshape.7) | copy-start | bytes 1179652
  222.3 147.8 %all-reduce.9.cloned.1.call-start = ((), (), s32[]{:S(2)}) async-start(), calls=%async_computation.7 | async-start | bytes 6291456 | tf_op jit(solution)/shard_map/psum | solution.py:234
  223.9 68.9 %copy-start.43 = (f32[768]{0:T(1024)}, f32[768]{0:T(1024)S(1)}, u32[]{:S(2)}) copy-start(f32[768]{0:T(1024)S(1)} %get-tuple-element.22) | copy-start | bytes 9220
  223.9 68.9 %copy-start.49 = (f32[768]{0:T(1024)}, f32[768]{0:T(1024)S(1)}, u32[]{:S(2)}) copy-start(f32[768]{0:T(1024)S(1)} %get-tuple-element.21) | copy-start | bytes 9220
  233.3 56.5 %copy-start.23 = (bf16[1,1024,768]{2,1,0:T(8,128)(2,1)S(1)}, bf16[1,1024,768]{2,1,0:T(8,128)(2,1)}, u32[]{:S(2)}) copy-start(bf16[1,1024,768]{2,1,0:T(8,128)(2,1)} %param.12) | copy-start | bytes 4718596
  301.5 160.0 %all-reduce.11.cloned.1.call-start = ((), (), s32[]{:S(2)}) async-start(), calls=%async_computation.8 | async-start | bytes 6291456 | tf_op jit(solution)/shard_map/psum | solution.py:257
  380.6 7.9 copy-start.5
  380.6 7.9 copy-start.45
  381.5 7.0 copy-start.26
  392.8 68.7 %copy-start.42 = (f32[1024]{0:T(1024)S(1)}, f32[1024]{0:T(1024)}, u32[]{:S(2)}) copy-start(f32[1024]{0:T(1024)} %copy-done.41) | copy-start | bytes 12292
  392.8 68.7 %copy-start.44 = (f32[768]{0:T(1024)S(1)}, f32[768]{0:T(1024)}, u32[]{:S(2)}) copy-start(f32[768]{0:T(1024)} %copy-done.43) | copy-start | bytes 9220
  392.8 68.7 %copy-start.46 = (f32[1024]{0:T(1024)S(1)}, f32[1024]{0:T(1024)}, u32[]{:S(2)}) copy-start(f32[1024]{0:T(1024)} %copy-done.45) | copy-start | bytes 12292
  392.8 269.5 %reduce-scatter.12.cloned.1.call-start = ((), (), s32[]{:S(2)}) async-start(), calls=%async_computation.10 | async-start | bytes 1966080 | tf_op jit(solution)/shard_map/reduce_scatter | solution.py:291
  393.6 73.3 %copy-start.51 = (f32[1024]{0:T(1024)S(1)}, f32[1024]{0:T(1024)}, u32[]{:S(2)}) copy-start(f32[1024]{0:T(1024)} %copy-done.50) | copy-start | bytes 12292
  473.4 7.2 copy-start.11
  548.4 119.6 %reduce-scatter.10.cloned.1.call-start = ((), (), s32[]{:S(2)}) async-start(), calls=%async_computation.9 | async-start | bytes 1966080 | tf_op jit(solution)/shard_map/reduce_scatter | solution.py:288
  632.4 99.9 %reduce-scatter.16.cloned.1.call-start = ((), (), s32[]{:S(2)}) async-start(), calls=%async_computation.15 | async-start | bytes 442368
  645.3 6.9 copy-start.56
  659.4 8.6 copy-start.36
  662.2 135.6 %reduce-scatter.18.cloned.1.call-start = ((), (), s32[]{:S(2)}) async-start(), calls=%async_computation.16 | async-start | bytes 663552
  664.6 178.1 %all-reduce.13.cloned.1.call-start = ((), (), s32[]{:S(2)}) async-start(), calls=%async_computation.11 | async-start | bytes 3145728 | tf_op jit(solution)/shard_map/psum | solution.py:302
  672.1 336.8 %reduce-scatter.14.cloned.1.call-start = ((), (), s32[]{:S(2)}) async-start(), calls=%async_computation.12 | async-start | bytes 10616832 | tf_op jit(solution)/shard_map/reduce_scatter | solution.py:312
  733.2 109.5 %copy-start.58 = (f32[6,96]{1,0:T(8,128)}, f32[6,96]{1,0:T(8,128)S(1)}, u32[]{:S(2)}) copy-start(f32[6,96]{1,0:T(8,128)S(1)} %copy.138) | copy-start | bytes 6916
  798.8 43.9 %copy-start.66 = (f32[1,144]{1,0:T(1,128)}, f32[1,144]{1,0:T(1,128)S(1)}, u32[]{:S(2)}) copy-start(f32[1,144]{1,0:T(1,128)S(1)} %copy.140) | copy-start | bytes 1732
  846.7 164.8 %copy-start.18 = (f32[24,96,96]{2,1,0:T(8,128)S(1)}, f32[24,96,96]{2,1,0:T(8,128)}, u32[]{:S(2)}) copy-start(f32[24,96,96]{2,1,0:T(8,128)} %param.16) | copy-start | bytes 2654212
  846.7 164.8 %copy-start.27 = (f32[24,96,96]{2,1,0:T(8,128)S(1)}, f32[24,96,96]{2,1,0:T(8,128)}, u32[]{:S(2)}) copy-start(f32[24,96,96]{2,1,0:T(8,128)} %param.22) | copy-start | bytes 2654212
  (61 other events, 180.4 us)
Sparse Core Ops, SparseCore 0:
  10.7 82.0 all-gather.5
  101.1 35.3 all-gather.9
  138.7 35.9 all-gather.7
  222.5 67.2 all-reduce.6
  301.6 68.5 all-reduce.8
  392.9 68.5 all-reduce.10
  548.5 35.4 reduce-scatter.11
  632.5 35.4 reduce-scatter.9
  671.3 61.0 reduce-scatter.15
  736.0 61.7 reduce-scatter.17
  800.8 41.8 all-reduce.12
  846.7 162.1 reduce-scatter.13
where the time goes:
time: 1030 us
  waiting for transfers between devices  597 us (58%)
  local copies, waits for them, and re-layouts  215 us (21%)
  other arithmetic  108 us (10%)
  matrix products  69.6 us (7%)
  blocking collectives  19.4 us (2%)
  between operations  16.1 us (2%)
    reduce_scatter x1, waiting for transfers between devices, per_device(): lax.psum_scatter(blocks_grad, ('shard', 'ctx'), scatter_dimension=0, tile...  162 us
    unnamed x14, waiting for transfers between devices  85.7 us
    all_gather x1, waiting for transfers between devices, per_device(): lax.all_gather(master_blocks.astype(jnp.bfloat16), ('shard', 'ctx'), axis...  83.2 us
    psum x1, waiting for transfers between devices, per_device(): lax.psum(jnp.dot(d_gate_low, wb_up.T, preferred_element_type=jnp.float32)...  67.9 us
    psum x1, waiting for transfers between devices, per_device(): lax.psum(jnp.dot(act_low, w_down, preferred_element_type=jnp.float32), 'tp')  67.8 us
    reshape x4, local copies, waits for them, and re-layouts, pick_blocks(): picked.reshape(clipped.shape[0], clipped.shape[1] * BLOCK, head_count, HEAD)  56.3 us
    psum x1, waiting for transfers between devices, per_device(): lax.psum(jnp.dot(attended_low, w_out, preferred_element_type=jnp.float32)...  52.6 us
    psum x1, waiting for transfers between devices, per_device(): lax.psum(jnp.dot(d_proj, wb_qkv.T, preferred_element_type=jnp.float32).as...  42.6 us
  transfers between devices with their start and end apart: 12, of which 11 were waited for; matrix products, arithmetic and copies ran while one was open for 19% of the time, Pallas kernels for 0%

commit v1 on v0

--- a/solution.py
+++ b/solution.py
@@ -16,6 +16,11 @@
 rate_vector = 0.001
 neg_large = -1e30
 high = lax.Precision.HIGHEST
+
+
+def recover_terms_for(chunk, lane_axis="tp"):
+    current_arr = lax.all_gather(chunk, lane_axis)
+    return jnp.sum(current_arr, axis=0)
 
 
 def layer_norm(values, gain, shift):
@@ -231,7 +236,7 @@
     gate_pre = jnp.dot(x_first_low, w_up, preferred_element_type=jnp.float32) + up_bias
     act_low = gelu_tanh(gate_pre).astype(jnp.bfloat16)
     ff_out = (
-        lax.psum(jnp.dot(act_low, w_down, preferred_element_type=jnp.float32), "tp")
+        recover_terms_for(jnp.dot(act_low, w_down, preferred_element_type=jnp.float32))
         + outer_vectors[1]
     )
     mixed_sum = x_first + ff_out

time: 1030 us -> 1060 us (1.029)
  waiting for transfers between devices: 597 us -> 611 us
    all_gather x0 -> x1, waiting for transfers between devices: none -> 81.4 us  [recover_terms_for(): current_arr = lax.all_gather(chunk, lane_axis)]
    psum x1 -> x0, waiting for transfers between devices: 67.8 us -> none  [per_device(): lax.psum(jnp.dot(act_low, w_down, preferred_element_type=jnp.float32), 'tp')]
where the time goes in v1:
time: 1060 us; the launch traced here: 1050 us
  waiting for transfers between devices  611 us (58%)
  local copies, waits for them, and re-layouts  215 us (20%)
  other arithmetic  116 us (11%)
  matrix products  69.6 us (7%)
  blocking collectives  19.5 us (2%)
  between operations  16.1 us (2%)
    reduce_scatter x1, waiting for transfers between devices, per_device(): lax.psum_scatter(blocks_grad, ('shard', 'ctx'), scatter_dimension=0, tile...  162 us
    unnamed x14, waiting for transfers between devices  85.7 us
    all_gather x1, waiting for transfers between devices, per_device(): lax.all_gather(master_blocks.astype(jnp.bfloat16), ('shard', 'ctx'), axis...  83.2 us
    all_gather x1, waiting for transfers between devices, recover_terms_for(): current_arr = lax.all_gather(chunk, lane_axis)  81.4 us
    psum x1, waiting for transfers between devices, per_device(): lax.psum(jnp.dot(d_gate_low, wb_up.T, preferred_element_type=jnp.float32)...  67.8 us
    reshape x4, local copies, waits for them, and re-layouts, pick_blocks(): picked.reshape(clipped.shape[0], clipped.shape[1] * BLOCK, head_count, HEAD)  56.3 us
    psum x1, waiting for transfers between devices, per_device(): lax.psum(jnp.dot(attended_low, w_out, preferred_element_type=jnp.float32)...  52.6 us
    psum x1, waiting for transfers between devices, per_device(): lax.psum(jnp.dot(d_proj, wb_qkv.T, preferred_element_type=jnp.float32).as...  42.6 us
  transfers between devices with their start and end apart: 12, of which 11 were waited for; matrix products, arithmetic and copies ran while one was open for 19% of the time, Pallas kernels for 0%

profile of v1, /device:TPU:0, one launch (start us, length us, event | category | flops | bytes accessed | tf_op | source)
XLA Modules:
  0.0 1048.8 jit_solution(4084512842213533725)
XLA Ops:
  9.6 83.2 %all-gather.8.cloned.1.call-done = bf16[192,96,96]{2,1,0:T(8,128)(2,1)} async-done(((bf16[24,96,96]{2,1,0:T(8,128)(2,1)}), bf16[192,96,96]{2,1,0:T(8,128)(2,1)}) %all-gather.8.cloned.1.call-update) | async-done | bytes 3538960 | tf_op jit(solution)/shard_map/all_gather | solution.py:170
  109.1 27.4 %all-gather.12.cloned.1.call-done = bf16[4096,192]{0,1:T(8,128)(2,1)} async-done(((bf16[1024,192]{0,1:T(8,128)(2,1)}), bf16[4096,192]{0,1:T(8,128)(2,1)}) %all-gather.12.cloned.1.call-update) | async-done | bytes 1572880 | tf_op jit(solution)/shard_map/all_gather | solution.py:192
  142.4 15.9 %reshape.560 = bf16[16,512,3,64]{3,2,1,0:T(4,128)(2,1)} reshape(bf16[128,64,192]{2,1,0:T(8,128)(2,1)} %gather_fusion.1) | data formatting | bytes 6291456 | tf_op jit(solution)/shard_map/reshape | solution.py:78
  158.4 12.2 %copy.106 = bf16[16,512,3,64]{1,3,2,0:T(8,128)(2,1)} copy(bf16[16,512,3,64]{3,2,1,0:T(4,128)(2,1)} %reshape.560) | data formatting | bytes 6291456 | tf_op jit(solution)/shard_map/reshape | solution.py:78
  170.6 4.1 all-gather.10.cloned.1.call-done
  180.5 15.9 %reshape.559 = bf16[16,512,3,64]{3,2,1,0:T(4,128)(2,1)} reshape(bf16[128,64,192]{2,1,0:T(8,128)(2,1)} %gather_fusion) | data formatting | bytes 6291456 | tf_op jit(solution)/shard_map/reshape | solution.py:78
  196.4 12.3 %copy.107 = bf16[16,512,3,64]{1,3,2,0:T(8,128)(2,1)} copy(bf16[16,512,3,64]{3,2,1,0:T(4,128)(2,1)} %reshape.559) | data formatting | bytes 6291456 | tf_op jit(solution)/shard_map/reshape | solution.py:78
  237.2 52.6 %all-reduce.6.cloned.1.call-done = f32[1024,768]{1,0:T(8,128)} async-done(((f32[1024,768]{1,0:T(8,128)}), f32[1024,768]{1,0:T(8,128)}) %all-reduce.6.cloned.1.call-update) | async-done | bytes 3145744 | tf_op jit(solution)/shard_map/psum | solution.py:230
  302.4 81.4 %all-gather.14.cloned.1.call-done = f32[4096,768]{1,0:T(8,128)} async-done(((f32[1024,768]{1,0:T(8,128)}), f32[4096,768]{1,0:T(8,128)}) %all-gather.14.cloned.1.call-update) | async-done | bytes 12582928 | tf_op jit(solution)/shard_map/all_gather | solution.py:22
  383.8 7.4 reduce_sum.183
  405.2 4.3 convert_reduce_fusion
  414.7 67.8 %all-reduce.8.cloned.1.call-done = f32[1024,768]{1,0:T(8,128)} async-done(((f32[1024,768]{1,0:T(8,128)}), f32[1024,768]{1,0:T(8,128)}) %all-reduce.8.cloned.1.call-update) | async-done | bytes 3145744 | tf_op jit(solution)/shard_map/psum | solution.py:262
  482.5 5.4 multiply_reduce_fusion.1
  494.4 7.2 fusion.20
  501.6 15.1 %copy.136 = f32[16,512,3,64]{3,2,1,0:T(4,128)} copy(f32[16,512,3,64]{1,3,2,0:T(8,128)} %fusion.20) | data formatting | bytes 12582912 | tf_op jit(solution)/shard_map/reshape | solution.py:137
  516.7 18.9 %reshape.554 = f32[128,64,192]{2,1,0:T(8,128)} reshape(f32[16,512,3,64]{3,2,1,0:T(4,128)} %copy.136) | data formatting | bytes 12582912 | tf_op jit(solution)/shard_map/reshape | solution.py:137
  538.0 26.2 %scatter_fusion.1 = f32[64,64,192]{2,1,0:T(8,128)} fusion(f32[64,64,192]{2,1,0:T(8,128)} %broadcast.358.clone, s32[128]{0:T(128)S(1)} %reshape.508, f32[128,64,192]{2,1,0:T(8,128)} %reshape.554), kind=kCustom, calls=%fused_computation.3 | custom fusion | flops 1572864 | bytes 18874880 | tf_op jit(solution)/shard_map/scatter-add | solution.py:137
  569.6 6.7 multiply_reduce_fusion
  585.5 15.1 %copy.135 = f32[16,512,3,64]{3,2,1,0:T(4,128)} copy(f32[16,512,3,64]{1,3,2,0:T(8,128)} %multiply_bitcast_fusion) | data formatting | bytes 12582912 | tf_op jit(solution)/shard_map/reshape | solution.py:132
  600.6 18.9 %reshape.553 = f32[128,64,192]{2,1,0:T(8,128)} reshape(f32[16,512,3,64]{3,2,1,0:T(4,128)} %copy.135) | data formatting | bytes 12582912 | tf_op jit(solution)/shard_map/reshape | solution.py:132
  622.0 26.2 %scatter_fusion = f32[64,64,192]{2,1,0:T(8,128)} fusion(f32[64,64,192]{2,1,0:T(8,128)} %broadcast.358.clone.1, s32[128]{0:T(128)S(1)} %reshape.508, f32[128,64,192]{2,1,0:T(8,128)} %reshape.553), kind=kCustom, calls=%fused_computation.2 | custom fusion | flops 1572864 | bytes 18874880 | tf_op jit(solution)/shard_map/scatter-add | solution.py:132
  653.7 4.3 fusion.58
  660.5 4.3 copy.127
  668.8 4.3 copy.126
  689.0 4.1 convolution_convert_fusion
  702.3 7.7 pad_maximum_fusion
  710.6 19.5 %pmax.7 = f32[3]{0:T(128)S(1)} all-reduce(f32[3]{0:T(128)S(1)} %broadcast_maximum_fusion), channel_id=1, replica_groups=mesh['shard'=2,'ctx'=4,'tp'=4] {'shard','ctx'}, use_global_device_ids=true, to_apply=%region_32.33 | all-reduce | flops 3 | bytes 24 | tf_op jit(solution)/shard_map/pmax | solution.py:244
  731.1 22.3 %reduce-scatter.16.cloned.1.call-done = f32[96,6]{1,0:T(8,128)} async-done(((f32[768,6]{1,0:T(8,128)}), f32[96,6]{1,0:T(8,128)}) %reduce-scatter.16.cloned.1.call-update) | async-done | bytes 2320
  755.6 63.3 %reduce-scatter.18.cloned.1.call-done = f32[144,1]{1,0:T(8,128)} async-done(((f32[1152,1]{1,0:T(8,128)}), f32[144,1]{1,0:T(8,128)}) %reduce-scatter.18.cloned.1.call-update) | async-done | bytes 592
  821.1 42.6 %all-reduce.10.cloned.1.call-done = bf16[1024,768]{1,0:T(8,128)(2,1)} async-done(((bf16[1024,768]{1,0:T(8,128)(2,1)}), bf16[1024,768]{1,0:T(8,128)(2,1)}) %all-reduce.10.cloned.1.call-update) | async-done | bytes 1572880 | tf_op jit(solution)/shard_map/psum | solution.py:307
  863.7 3.9 fusion.26
  867.7 162.3 %reduce-scatter.14.cloned.1.call-done = f32[24,96,96]{2,1,0:T(8,128)} async-done(((f32[192,96,96]{2,1,0:T(8,128)}), f32[24,96,96]{2,1,0:T(8,128)}) %reduce-scatter.14.cloned.1.call-update) | async-done | bytes 884752 | tf_op jit(solution)/shard_map/reduce_scatter | solution.py:317
  (318 shorter events, 170.1 us)
Async XLA Ops:
  7.2 1022.7 %copy-start = (f32[24,96,96]{2,1,0:T(8,128)S(1)}, f32[24,96,96]{2,1,0:T(8,128)}, u32[]{:S(2)}) copy-start(f32[24,96,96]{2,1,0:T(8,128)} %param.21) | copy-start | bytes 2654212
  7.2 85.6 %all-gather.8.cloned.1.call-start = ((), (), s32[]{:S(2)}) async-start(), calls=%async_computation.5 | async-start | bytes 5308416 | tf_op jit(solution)/shard_map/all_gather | solution.py:170
  9.5 127.0 %all-gather.12.cloned.1.call-start = ((), (), s32[]{:S(2)}) async-start(), calls=%async_computation.13 | async-start | bytes 1966080 | tf_op jit(solution)/shard_map/all_gather | solution.py:192
  100.9 6.9 slice-start.1
  101.0 73.7 %all-gather.10.cloned.1.call-start = ((), (), s32[]{:S(2)}) async-start(), calls=%async_computation.12 | async-start | bytes 1966080 | tf_op jit(solution)/shard_map/all_gather | solution.py:193
  103.4 186.4 %all-reduce.6.cloned.1.call-start = ((), (), s32[]{:S(2)}) async-start(), calls=%async_computation.6 | async-start | bytes 6291456 | tf_op jit(solution)/shard_map/psum | solution.py:230
  196.4 12.3 %copy-start.12 = (bf16[16,64,3,64]{1,0,3,2:T(8,128)(2,1)S(1)}, bf16[16,64,3,64]{1,0,3,2:T(8,128)(2,1)}, u32[]{:S(2)}) copy-start(bf16[16,64,3,64]{1,0,3,2:T(8,128)(2,1)} %reshape_squeeze_reshape.7) | copy-start | bytes 1179652
  222.3 161.5 %all-gather.14.cloned.1.call-start = ((), (), s32[]{:S(2)}) async-start(), calls=%async_computation.14 | async-start | bytes 15728640 | tf_op jit(solution)/shard_map/all_gather | solution.py:22
  223.9 68.9 %copy-start.43 = (f32[768]{0:T(1024)}, f32[768]{0:T(1024)S(1)}, u32[]{:S(2)}) copy-start(f32[768]{0:T(1024)S(1)} %get-tuple-element.22) | copy-start | bytes 9220
  223.9 68.9 %copy-start.49 = (f32[768]{0:T(1024)}, f32[768]{0:T(1024)S(1)}, u32[]{:S(2)}) copy-start(f32[768]{0:T(1024)S(1)} %get-tuple-element.21) | copy-start | bytes 9220
  233.3 56.5 %copy-start.23 = (bf16[1,1024,768]{2,1,0:T(8,128)(2,1)S(1)}, bf16[1,1024,768]{2,1,0:T(8,128)(2,1)}, u32[]{:S(2)}) copy-start(bf16[1,1024,768]{2,1,0:T(8,128)(2,1)} %param.12) | copy-start | bytes 4718596
  301.5 181.0 %all-reduce.8.cloned.1.call-start = ((), (), s32[]{:S(2)}) async-start(), calls=%async_computation.7 | async-start | bytes 6291456 | tf_op jit(solution)/shard_map/psum | solution.py:262
  401.6 7.9 copy-start.5
  401.6 7.9 copy-start.45
  402.6 7.0 copy-start.26
  413.9 68.7 %copy-start.42 = (f32[1024]{0:T(1024)S(1)}, f32[1024]{0:T(1024)}, u32[]{:S(2)}) copy-start(f32[1024]{0:T(1024)} %copy-done.41) | copy-start | bytes 12292
  413.9 68.7 %copy-start.44 = (f32[768]{0:T(1024)S(1)}, f32[768]{0:T(1024)}, u32[]{:S(2)}) copy-start(f32[768]{0:T(1024)} %copy-done.43) | copy-start | bytes 9220
  413.9 68.6 %copy-start.46 = (f32[1024]{0:T(1024)S(1)}, f32[1024]{0:T(1024)}, u32[]{:S(2)}) copy-start(f32[1024]{0:T(1024)} %copy-done.45) | copy-start | bytes 12292
  413.9 269.4 %reduce-scatter.12.cloned.1.call-start = ((), (), s32[]{:S(2)}) async-start(), calls=%async_computation.9 | async-start | bytes 1966080 | tf_op jit(solution)/shard_map/reduce_scatter | solution.py:296
  414.6 73.2 %copy-start.51 = (f32[1024]{0:T(1024)S(1)}, f32[1024]{0:T(1024)}, u32[]{:S(2)}) copy-start(f32[1024]{0:T(1024)} %copy-done.50) | copy-start | bytes 12292
  494.4 7.2 copy-start.11
  569.4 119.6 %reduce-scatter.10.cloned.1.call-start = ((), (), s32[]{:S(2)}) async-start(), calls=%async_computation.8 | async-start | bytes 1966080 | tf_op jit(solution)/shard_map/reduce_scatter | solution.py:293
  653.4 99.9 %reduce-scatter.16.cloned.1.call-start = ((), (), s32[]{:S(2)}) async-start(), calls=%async_computation.15 | async-start | bytes 442368
  666.2 6.9 copy-start.56
  680.4 8.6 copy-start.36
  683.2 135.6 %reduce-scatter.18.cloned.1.call-start = ((), (), s32[]{:S(2)}) async-start(), calls=%async_computation.16 | async-start | bytes 663552
  685.6 178.2 %all-reduce.10.cloned.1.call-start = ((), (), s32[]{:S(2)}) async-start(), calls=%async_computation.10 | async-start | bytes 3145728 | tf_op jit(solution)/shard_map/psum | solution.py:307
  693.1 336.8 %reduce-scatter.14.cloned.1.call-start = ((), (), s32[]{:S(2)}) async-start(), calls=%async_computation.11 | async-start | bytes 10616832 | tf_op jit(solution)/shard_map/reduce_scatter | solution.py:317
  754.2 109.6 %copy-start.58 = (f32[6,96]{1,0:T(8,128)}, f32[6,96]{1,0:T(8,128)S(1)}, u32[]{:S(2)}) copy-start(f32[6,96]{1,0:T(8,128)S(1)} %copy.138) | copy-start | bytes 6916
  819.8 43.9 %copy-start.66 = (f32[1,144]{1,0:T(1,128)}, f32[1,144]{1,0:T(1,128)S(1)}, u32[]{:S(2)}) copy-start(f32[1,144]{1,0:T(1,128)S(1)} %copy.140) | copy-start | bytes 1732
  867.7 164.8 %copy-start.18 = (f32[24,96,96]{2,1,0:T(8,128)S(1)}, f32[24,96,96]{2,1,0:T(8,128)}, u32[]{:S(2)}) copy-start(f32[24,96,96]{2,1,0:T(8,128)} %param.16) | copy-start | bytes 2654212
  867.7 164.8 %copy-start.27 = (f32[24,96,96]{2,1,0:T(8,128)S(1)}, f32[24,96,96]{2,1,0:T(8,128)}, u32[]{:S(2)}) copy-start(f32[24,96,96]{2,1,0:T(8,128)} %param.22) | copy-start | bytes 2654212
  (61 other events, 180.4 us)
Sparse Core Ops, SparseCore 0:
  10.7 82.0 all-gather.7
  101.1 35.3 all-gather.11
  138.7 35.9 all-gather.9
  222.5 67.2 all-reduce.5
  301.6 82.1 all-gather.13
  414.0 68.4 all-reduce.7
  569.5 35.4 reduce-scatter.11
  653.5 35.4 reduce-scatter.9
  692.2 61.0 reduce-scatter.15
  757.0 61.7 reduce-scatter.17
  821.8 41.8 all-reduce.9
  867.7 162.1 reduce-scatter.13
